TPU v7x, 256 devices: a whole 4x4x8 slice. The times are simulated.
256 devices in a mesh: ctx: 32 (over z, y), tp: 8 (over x, core).
Axes of the slice: x: 4, y: 4, z: 8, core: 2. Of those that a mesh axis runs over, the one named last changes fastest.
Arguments:
- tokens: bfloat16 [24576, 4096], P(('ctx', 'tp')), may hold values from -6 to 6
- norm_gain: float32 [4096], replicated, may hold values from 0.1 to 1.9
- w_qkv: bfloat16 [4096, 8192], P('ctx', 'tp'), may hold values from -0.09375 to 0.09375
- w_out: bfloat16 [4096, 4096], P('tp', 'ctx'), may hold values from -0.09375 to 0.09375
- head_gain: float32 [4096], P('tp'), may hold values from 0.1 to 1.9
- input_codes: int32 [8, 24576], P('tp', 'ctx'), may hold values from -4 to 4
- forget_codes: int32 [8, 24576], P('tp', 'ctx'), may hold values from -24 to 4
- forget_bias: float32 [8], P('tp'), may hold values from 3 to 13.5, as said below
- document_begin_flags: int32 [24576], P('ctx'), may hold values 0 or 1
Outputs:
- mixed: bfloat16 [24576, 4096], P(('ctx', 'tp'))
Inputs may be any that keep to these rules, and one draw needn't show every extreme that they name: `forget_bias`: a bias for each head.
All inputs are finite; a program needn't handle non-finite values. No bound on the sum of `document_begin_flags` on one device may be relied on, other than what follows from the above.
Results may differ from a plain program's by a relative error of at most 0.017.
Values may be sent and summed in bfloat16 or wider, within the bound.
A program may use at most 64 MiB of HBM per device.

v0:
```python
import jax
import jax.numpy as jnp
from jax import lax
from jax.sharding import PartitionSpec as P

DK = 256
DV = 512
EPSILON = 1e-06
FORGET_STEP = 0.5
INPUT_STEP = 0.5


def carried_in(passing, state, axis):
    count = lax.axis_size(axis)
    if count == 1:
        return jnp.zeros_like(state)
    heads, rows, width = state.shape
    pad = 16

    def shifted(decay, total, k):
        high = decay.astype(jnp.bfloat16)
        low = (decay - high.astype(jnp.float32)).astype(jnp.bfloat16)
        extra = jnp.zeros((heads, pad, width), jnp.bfloat16)
        extra = extra.at[:, 0, 0].set(high).at[:, 0, 1].set(low)
        message = jnp.concatenate([total.astype(jnp.bfloat16), extra], axis=1)
        pairs = [(i, i + k) for i in range(count - k)]
        got = lax.ppermute(message, axis, pairs)
        got_decay = got[:, rows, 0].astype(jnp.float32) + got[:, rows, 1].astype(jnp.float32)
        return (got_decay, got[:, :rows].astype(jnp.float32))

    decay, total = shifted(passing, state, 1)
    if count > 2:
        decay_far, total_far = shifted(passing, state, 2)
        total = decay[:, None, None] * total_far + total
        decay = decay * decay_far
    k = 2
    while k < count:
        decay_far, total_far = shifted(decay, total, k)
        total = decay[:, None, None] * total_far + total
        decay = decay * decay_far
        k *= 2
    return total


def rms_rows(embedded_entries, norm_gain):
    token_float = embedded_entries.astype(jnp.float32)
    moment = jnp.mean(token_float * token_float, axis=1, keepdims=True)
    return (token_float * lax.rsqrt(moment + EPSILON) * norm_gain).astype(jnp.bfloat16)


def local_terms(queries, key_rows, values, log_forget, input_gate, starts):
    length = queries.shape[0]
    scaling = queries.shape[1] ** (-0.5)
    segment = jnp.cumsum(starts)
    levels = jnp.cumsum(log_forget)
    position = jnp.arange(length)
    allowed = (position[:, None] >= position[None, :]) & (segment[:, None] == segment[None, :])
    decays = jnp.where(
        allowed,
        jnp.exp(jnp.minimum(levels[:, None] - levels[None, :], 0.0) + input_gate[None, :]),
        0.0,
    )
    scores = jnp.dot(queries, key_rows.T, preferred_element_type=jnp.float32) * scaling
    weights = (scores * decays).astype(jnp.bfloat16)
    inner_part = jnp.dot(weights, values, preferred_element_type=jnp.float32)
    last_level = levels[-1]
    last_seg = segment[-1]
    keeping = jnp.where(segment == last_seg, jnp.exp(last_level - levels + input_gate), 0.0)
    weighted = (key_rows.astype(jnp.float32) * keeping[:, None]).astype(jnp.bfloat16)
    local_state = lax.dot_general(
        weighted, values, (((0,), (0,)), ((), ())), preferred_element_type=jnp.float32
    )
    passing = jnp.where(last_seg == 0, jnp.exp(last_level), 0.0)
    carried = jnp.where(segment == 0, jnp.exp(levels), 0.0) * scaling
    return (inner_part, local_state, passing, carried)


def apply_state(queries, carried, incoming):
    lifted = queries.astype(jnp.float32) * carried[:, None]
    return jnp.dot(
        lifted, incoming, precision=lax.Precision.HIGHEST, preferred_element_type=jnp.float32
    )


def head_norm(head_out, gain):
    centre = jnp.mean(head_out, axis=1, keepdims=True)
    shifted = head_out - centre
    spread = jnp.mean(shifted * shifted, axis=1, keepdims=True)
    return (shifted * lax.rsqrt(spread + EPSILON) * gain).astype(jnp.bfloat16)


def local(
    tokens,
    norm_gain,
    w_qkv,
    w_out,
    head_gain,
    input_codes,
    forget_codes,
    forget_bias,
    document_begin_flags,
):
    normed = rms_rows(tokens, norm_gain)
    group = lax.axis_size("tp")
    copies = jnp.broadcast_to(normed[None], (group,) + normed.shape)
    every_row_list = lax.all_to_all(copies, "tp", 0, 0, tiled=True).reshape(-1, normed.shape[1])
    parameter_collection = lax.all_gather(w_qkv, "ctx", axis=0, tiled=True)
    rows_combined = jnp.dot(
        every_row_list, parameter_collection, preferred_element_type=jnp.float32
    )
    rows_combined = rows_combined.astype(jnp.bfloat16)
    heads_here = forget_bias.shape[0]
    stride = 2 * DK + DV
    query_list, inner_list, state_list, passing_list, carried_list = ([], [], [], [], [])
    attention_slot_number = 0
    offset = attention_slot_number * stride
    queries = rows_combined[:, offset : offset + DK]
    key_rows = rows_combined[:, offset + DK : offset + 2 * DK]
    values = rows_combined[:, offset + 2 * DK : offset + stride]
    log_forget = jax.nn.log_sigmoid(
        FORGET_STEP * forget_codes[attention_slot_number].astype(jnp.float32)
        + forget_bias[attention_slot_number]
    )
    input_gate = INPUT_STEP * input_codes[attention_slot_number].astype(jnp.float32)
    inner_part, local_state, passing, carried = local_terms(
        queries, key_rows, values, log_forget, input_gate, document_begin_flags
    )
    query_list.append(queries)
    inner_list.append(inner_part)
    state_list.append(local_state)
    passing_list.append(passing)
    carried_list.append(carried)
    incoming = carried_in(jnp.stack(passing_list), jnp.stack(state_list), "ctx")
    attention_slot_number = 0
    head_out = inner_list[attention_slot_number] + apply_state(
        query_list[attention_slot_number],
        carried_list[attention_slot_number],
        incoming[attention_slot_number],
    )
    normed_heads = head_norm(head_out, head_gain)
    out_columns = lax.all_gather(w_out, "ctx", axis=1, tiled=True)
    summed = lax.psum_scatter(
        jnp.dot(normed_heads, out_columns, preferred_element_type=jnp.float32).astype(jnp.bfloat16),
        "tp",
        scatter_dimension=0,
        tiled=True,
    ).astype(jnp.float32)
    return (tokens.astype(jnp.float32) + summed).astype(jnp.bfloat16)


def solution(mesh):
    placed = (
        P(("ctx", "tp"), None),
        P(),
        P("ctx", "tp"),
        P("tp", "ctx"),
        P("tp"),
        P("tp", "ctx"),
        P("tp", "ctx"),
        P("tp"),
        P("ctx"),
    )
    return jax.shard_map(
        local, mesh=mesh, in_specs=placed, out_specs=P(("ctx", "tp"), None), check_vma=False
    )
```

profile of v0, /device:TPU:1, one launch (start us, length us, event | category | flops | bytes accessed | tf_op | source)
XLA Modules:
  0.0 284.2 jit_solution(16675667116050032039)
XLA Ops:
  7.3 1.4 fusion.1
  9.7 3.3 %broadcast_in_dim.5 = bf16[8,96,4096]{2,1,0:T(8,128)(2,1)} broadcast(bf16[96,4096]{1,0:T(8,128)(2,1)S(1)} %fusion.3), dimensions={1,2} | broadcast | bytes 7077888 | tf_op jit(solution)/shard_map/broadcast_in_dim | solution.py:105
  13.0 8.0 %all-to-all-start = ((bf16[8,96,4096]{2,1,0:T(8,128)(2,1)}), bf16[8,96,4096]{2,1,0:T(8,128)(2,1)}, u32[]{:S(2)}, u32[]{:S(2)}) async-start(bf16[8,96,4096]{2,1,0:T(8,128)(2,1)} %broadcast_in_dim.5), calls=%async_computation | async-start | bytes 12582912 | tf_op jit(solution)/shard_map/all_to_all | solution.py:106
  29.4 63.0 %all-to-all-done = bf16[8,96,4096]{2,1,0:T(8,128)(2,1)} async-done(((bf16[8,96,4096]{2,1,0:T(8,128)(2,1)}), bf16[8,96,4096]{2,1,0:T(8,128)(2,1)}, u32[]{:S(2)}, u32[]{:S(2)}) %all-to-all-start) | async-done | bytes 6291488 | tf_op jit(solution)/shard_map/all_to_all | solution.py:106
  92.5 19.3 %all-gather.3.cloned.1.call-done = bf16[4096,1024]{1,0:T(8,128)(2,1)} async-done(((bf16[128,1024]{1,0:T(8,128)(2,1)}), bf16[4096,1024]{1,0:T(8,128)(2,1)}) %all-gather.3.cloned.1.call-update) | async-done | bytes 8388624 | tf_op jit(solution)/shard_map/all_gather | solution.py:107
  111.7 10.9 %convolution_convert_fusion.1 = bf16[768,1024]{1,0:T(8,128)(2,1)S(1)} fusion(bf16[768,4096]{1,0:T(8,128)(2,1)} %bitcast, bf16[4096,1024]{1,0:T(8,128)(2,1)} %all-gather.3.cloned.1.call-done), kind=kOutput, calls=%fused_computation.7 | convolution fusion | flops 6443237376 | bytes 16252928 | tf_op jit(solution)/shard_map/dot_general | solution.py:108
  123.3 1.9 collective-permute-start
  125.1 3.7 %collective-permute-start.1 = (bf16[1,272,512]{2,1,0:T(8,128)(2,1)S(1)}, bf16[1,272,512]{2,1,0:T(8,128)(2,1)S(1)}, u32[]{:S(2)}, u32[]{:S(2)}) collective-permute-start(bf16[1,272,512]{2,1,0:T(8,128)(2,1)S(1)} %pad_maximum_fusion), channel_id=1, source_target_pairs={{0,16},{8,24},{16,32},{24,40},{32,48},{40,56},{48,64},{56,72},{64,... | collective-permute-start | bytes 835592 | tf_op jit(solution)/shard_map/ppermute | solution.py:27
  128.9 2.4 collective-permute-done
  133.1 4.3 %collective-permute-done.1 = bf16[1,272,512]{2,1,0:T(8,128)(2,1)S(1)} collective-permute-done((bf16[1,272,512]{2,1,0:T(8,128)(2,1)S(1)}, bf16[1,272,512]{2,1,0:T(8,128)(2,1)S(1)}, u32[]{:S(2)}, u32[]{:S(2)}) %collective-permute-start.1) | collective-permute-done | bytes 278560 | tf_op jit(solution)/shard_map/ppermute | solution.py:27
  140.7 5.6 %collective-permute-start.2 = (bf16[1,272,512]{2,1,0:T(8,128)(2,1)S(1)}, bf16[1,272,512]{2,1,0:T(8,128)(2,1)S(1)}, u32[]{:S(2)}, u32[]{:S(2)}) collective-permute-start(bf16[1,272,512]{2,1,0:T(8,128)(2,1)S(1)} %pad_maximum_fusion.1), channel_id=1, source_target_pairs={{0,16},{8,24},{16,32},{24,40},{32,48},{40,56},{48,64},{56,72},{64,... | collective-permute-start | bytes 835592 | tf_op jit(solution)/shard_map/ppermute | solution.py:27
  146.3 4.9 %collective-permute-done.2 = bf16[1,272,512]{2,1,0:T(8,128)(2,1)S(1)} collective-permute-done((bf16[1,272,512]{2,1,0:T(8,128)(2,1)S(1)}, bf16[1,272,512]{2,1,0:T(8,128)(2,1)S(1)}, u32[]{:S(2)}, u32[]{:S(2)}) %collective-permute-start.2) | collective-permute-done | bytes 278560 | tf_op jit(solution)/shard_map/ppermute | solution.py:27
  154.6 4.7 %collective-permute-start.3 = (bf16[1,272,512]{2,1,0:T(8,128)(2,1)S(1)}, bf16[1,272,512]{2,1,0:T(8,128)(2,1)S(1)}, u32[]{:S(2)}, u32[]{:S(2)}) collective-permute-start(bf16[1,272,512]{2,1,0:T(8,128)(2,1)S(1)} %pad_maximum_fusion.2), channel_id=1, source_target_pairs={{0,32},{8,40},{16,48},{24,56},{32,64},{40,72},{48,80},{56,88},{64,... | collective-permute-start | bytes 835592 | tf_op jit(solution)/shard_map/ppermute | solution.py:27
  159.3 3.5 %collective-permute-done.3 = bf16[1,272,512]{2,1,0:T(8,128)(2,1)S(1)} collective-permute-done((bf16[1,272,512]{2,1,0:T(8,128)(2,1)S(1)}, bf16[1,272,512]{2,1,0:T(8,128)(2,1)S(1)}, u32[]{:S(2)}, u32[]{:S(2)}) %collective-permute-start.3) | collective-permute-done | bytes 278560 | tf_op jit(solution)/shard_map/ppermute | solution.py:27
  166.2 5.7 %collective-permute-start.4 = (bf16[1,272,512]{2,1,0:T(8,128)(2,1)S(1)}, bf16[1,272,512]{2,1,0:T(8,128)(2,1)S(1)}, u32[]{:S(2)}, u32[]{:S(2)}) collective-permute-start(bf16[1,272,512]{2,1,0:T(8,128)(2,1)S(1)} %pad_maximum_fusion.3), channel_id=1, source_target_pairs={{0,64},{8,72},{16,80},{24,88},{32,96},{40,104},{48,112},{56,120},{... | collective-permute-start | bytes 835592 | tf_op jit(solution)/shard_map/ppermute | solution.py:27
  171.9 4.0 %collective-permute-done.4 = bf16[1,272,512]{2,1,0:T(8,128)(2,1)S(1)} collective-permute-done((bf16[1,272,512]{2,1,0:T(8,128)(2,1)S(1)}, bf16[1,272,512]{2,1,0:T(8,128)(2,1)S(1)}, u32[]{:S(2)}, u32[]{:S(2)}) %collective-permute-start.4) | collective-permute-done | bytes 278560 | tf_op jit(solution)/shard_map/ppermute | solution.py:27
  179.4 17.8 %collective-permute-start.5 = (bf16[1,272,512]{2,1,0:T(8,128)(2,1)S(1)}, bf16[1,272,512]{2,1,0:T(8,128)(2,1)S(1)}, u32[]{:S(2)}, u32[]{:S(2)}) collective-permute-start(bf16[1,272,512]{2,1,0:T(8,128)(2,1)S(1)} %pad_maximum_fusion.4), channel_id=1, source_target_pairs={{0,128},{8,136},{16,144},{24,152},{32,160},{40,168},{48,176},{56,1... | collective-permute-start | bytes 835592 | tf_op jit(solution)/shard_map/ppermute | solution.py:27
  197.2 4.0 %fusion.5 = f32[768,512]{0,1:T(8,128)} fusion(f32[768]{0:T(1024)S(1)} %multiply_reduce_fusion.1, f32[768]{0:T(1024)S(1)} %get-tuple-element.143, s32[768]{0:T(1024)S(1)} %get-tuple-element.142, bf16[768,1024]{1,0:T(8,128)(2,1)} %copy-done.3), kind=kOutput, calls=%fused_computation.15 | convolution fusion | flops 911867904 | bytes 3166208 | tf_op jit(solution)/shard_map/dot_general | solution.py:65
  201.2 1.8 collective-permute-done.5
  203.7 3.6 %fusion.52 = (f32[768]{0:T(1024)S(1)}, f32[768,512]{0,1:T(8,128)S(1)}) fusion(f32[768,512]{0,1:T(8,128)} %fusion.5, bf16[1,272,512]{2,1,0:T(8,128)(2,1)} %copy-done.2, f32[]{:T(128)} %bitcast.26, bf16[1,272,512]{2,1,0:T(8,128)(2,1)S(1)} %collective-permute-done.3, f32[]{:T(128)} %bitcast.22, bf16[1,272,512]{2,1,0:T(8,128)(2,1)} %copy-done.1, f32[]{:T(128)} %bitcast.27, ...), kind=kOutput, calls=%fused_computation.85 | convolution fusion | flops 1211235584 | bytes 5121536 | tf_op jit(solution)/shard_map/dot_general | solution.py:80
  207.6 10.5 %all-gather.5.cloned.1.call-done = bf16[512,4096]{1,0:T(8,128)(2,1)} async-done(((bf16[512,128]{1,0:T(8,128)(2,1)}), bf16[512,4096]{1,0:T(8,128)(2,1)}) %all-gather.5.cloned.1.call-update) | async-done | bytes 4194320 | tf_op jit(solution)/shard_map/all_gather | solution.py:141
  218.0 7.7 %convolution_convert_fusion = bf16[768,4096]{1,0:T(8,128)(2,1)} fusion(bf16[512,4096]{1,0:T(8,128)(2,1)} %all-gather.5.cloned.1.call-done, f32[768,512]{0,1:T(8,128)S(1)} %get-tuple-element.157, f32[512]{0:T(512)S(1)} %copy-done.7, f32[768]{0:T(1024)S(1)} %add_rsqrt_fusion, f32[768]{0:T(1024)S(1)} %broadcast_multiply_fusion), kind=kOutput, calls=%fused_computation | convolution fusion | flops 3225944064 | bytes 12066816 | tf_op jit(solution)/shard_map/dot_general | solution.py:143
  225.8 49.7 %reduce-scatter.2.cloned.1.call-done = bf16[96,4096]{1,0:T(8,128)(2,1)} async-done(((bf16[768,4096]{1,0:T(8,128)(2,1)}), bf16[96,4096]{1,0:T(8,128)(2,1)}) %reduce-scatter.2.cloned.1.call-update) | async-done | bytes 786448 | tf_op jit(solution)/shard_map/reduce_scatter | solution.py:142
  275.5 2.2 fusion.4
  (69 shorter events, 18.4 us)
Async XLA Ops:
  6.5 2.1 copy-start
  6.5 105.2 %all-gather.3.cloned.1.call-start = ((), (), s32[]{:S(2)}) async-start(), calls=%async_computation.2 | async-start | bytes 8650752 | tf_op jit(solution)/shard_map/all_gather | solution.py:107
  13.0 9.5 %copy-start.6 = (s32[1,768]{1,0:T(1,128)S(1)}, s32[1,768]{1,0:T(1,128)}, u32[]{:S(2)}) copy-start(s32[1,768]{1,0:T(1,128)} %param.39) | copy-start | bytes 9220
  13.0 9.9 %copy-start.4 = (s32[768]{0:T(1024)S(1)}, s32[768]{0:T(1024)}, u32[]{:S(2)}) copy-start(s32[768]{0:T(1024)} %param.41) | copy-start | bytes 9220
  13.0 15.1 %copy-start.5 = (s32[1,768]{1,0:T(1,128)S(1)}, s32[1,768]{1,0:T(1,128)}, u32[]{:S(2)}) copy-start(s32[1,768]{1,0:T(1,128)} %param.38) | copy-start | bytes 9220
  13.0 79.4 %all-to-all-start = ((bf16[8,96,4096]{2,1,0:T(8,128)(2,1)}), bf16[8,96,4096]{2,1,0:T(8,128)(2,1)}, u32[]{:S(2)}, u32[]{:S(2)}) async-start(bf16[8,96,4096]{2,1,0:T(8,128)(2,1)} %broadcast_in_dim.5), calls=%async_computation | async-start | bytes 12582912 | tf_op jit(solution)/shard_map/all_to_all | solution.py:106
  21.1 197.0 %all-gather.5.cloned.1.call-start = ((), (), s32[]{:S(2)}) async-start(), calls=%async_computation.3 | async-start | bytes 4325376 | tf_op jit(solution)/shard_map/all_gather | solution.py:141
  21.8 253.7 %reduce-scatter.2.cloned.1.call-start = ((), (), s32[]{:S(2)}) async-start(), calls=%async_computation.4 | async-start | bytes 7077888 | tf_op jit(solution)/shard_map/reduce_scatter | solution.py:142
  122.6 14.7 %copy-start.3 = (bf16[768,1024]{1,0:T(8,128)(2,1)}, bf16[768,1024]{1,0:T(8,128)(2,1)S(1)}, u32[]{:S(2)}) copy-start(bf16[768,1024]{1,0:T(8,128)(2,1)S(1)} %convolution_convert_fusion.1) | copy-start | bytes 4718596
  123.3 8.0 %collective-permute-start = (bf16[1,272,512]{2,1,0:T(8,128)(2,1)S(1)}, bf16[1,272,512]{2,1,0:T(8,128)(2,1)S(1)}, u32[]{:S(2)}, u32[]{:S(2)}) collective-permute-start(bf16[1,272,512]{2,1,0:T(8,128)(2,1)S(1)} %pad_maximum_fusion), channel_id=1, source_target_pairs={{0,8},{8,16},{16,24},{24,32},{32,40},{40,48},{48,56},{56,64},{64,7... | collective-permute-start | bytes 835592 | tf_op jit(solution)/shard_map/ppermute | solution.py:27
  125.1 12.3 %collective-permute-start.1 = (bf16[1,272,512]{2,1,0:T(8,128)(2,1)S(1)}, bf16[1,272,512]{2,1,0:T(8,128)(2,1)S(1)}, u32[]{:S(2)}, u32[]{:S(2)}) collective-permute-start(bf16[1,272,512]{2,1,0:T(8,128)(2,1)S(1)} %pad_maximum_fusion), channel_id=1, source_target_pairs={{0,16},{8,24},{16,32},{24,40},{32,48},{40,56},{48,64},{56,72},{64,... | collective-permute-start | bytes 835592 | tf_op jit(solution)/shard_map/ppermute | solution.py:27
  140.7 10.5 %collective-permute-start.2 = (bf16[1,272,512]{2,1,0:T(8,128)(2,1)S(1)}, bf16[1,272,512]{2,1,0:T(8,128)(2,1)S(1)}, u32[]{:S(2)}, u32[]{:S(2)}) collective-permute-start(bf16[1,272,512]{2,1,0:T(8,128)(2,1)S(1)} %pad_maximum_fusion.1), channel_id=1, source_target_pairs={{0,16},{8,24},{16,32},{24,40},{32,48},{40,56},{48,64},{56,72},{64,... | collective-permute-start | bytes 835592 | tf_op jit(solution)/shard_map/ppermute | solution.py:27
  154.6 8.2 %collective-permute-start.3 = (bf16[1,272,512]{2,1,0:T(8,128)(2,1)S(1)}, bf16[1,272,512]{2,1,0:T(8,128)(2,1)S(1)}, u32[]{:S(2)}, u32[]{:S(2)}) collective-permute-start(bf16[1,272,512]{2,1,0:T(8,128)(2,1)S(1)} %pad_maximum_fusion.2), channel_id=1, source_target_pairs={{0,32},{8,40},{16,48},{24,56},{32,64},{40,72},{48,80},{56,88},{64,... | collective-permute-start | bytes 835592 | tf_op jit(solution)/shard_map/ppermute | solution.py:27
  166.2 9.7 %collective-permute-start.4 = (bf16[1,272,512]{2,1,0:T(8,128)(2,1)S(1)}, bf16[1,272,512]{2,1,0:T(8,128)(2,1)S(1)}, u32[]{:S(2)}, u32[]{:S(2)}) collective-permute-start(bf16[1,272,512]{2,1,0:T(8,128)(2,1)S(1)} %pad_maximum_fusion.3), channel_id=1, source_target_pairs={{0,64},{8,72},{16,80},{24,88},{32,96},{40,104},{48,112},{56,120},{... | collective-permute-start | bytes 835592 | tf_op jit(solution)/shard_map/ppermute | solution.py:27
  175.9 25.3 %copy-start.1 = (bf16[1,272,512]{2,1,0:T(8,128)(2,1)}, bf16[1,272,512]{2,1,0:T(8,128)(2,1)S(1)}, u32[]{:S(2)}) copy-start(bf16[1,272,512]{2,1,0:T(8,128)(2,1)S(1)} %collective-permute-done.4) | copy-start | bytes 835588
  179.4 23.6 %collective-permute-start.5 = (bf16[1,272,512]{2,1,0:T(8,128)(2,1)S(1)}, bf16[1,272,512]{2,1,0:T(8,128)(2,1)S(1)}, u32[]{:S(2)}, u32[]{:S(2)}) collective-permute-start(bf16[1,272,512]{2,1,0:T(8,128)(2,1)S(1)} %pad_maximum_fusion.4), channel_id=1, source_target_pairs={{0,128},{8,136},{16,144},{24,152},{32,160},{40,168},{48,176},{56,1... | collective-permute-start | bytes 835592 | tf_op jit(solution)/shard_map/ppermute | solution.py:27
  203.0 0.7 copy-start.2
  207.3 10.7 %copy-start.7 = (f32[512]{0:T(512)S(1)}, f32[512]{0:T(512)}, u32[]{:S(2)}) copy-start(f32[512]{0:T(512)} %param.37) | copy-start | bytes 6148
Sparse Core Ops, SparseCore 0:
  9.9 101.7 all-gather.2
  114.2 103.7 all-gather.4
  225.9 49.5 reduce-scatter.1
where the time goes:
time: 285 us; the launch traced here: 284 us
  waiting for transfers between devices  165 us (58%)
  starting transfers between devices  47.5 us (17%)
  matrix products  26.8 us (9%)
  between operations  21.9 us (8%)
  local copies, waits for them, and re-layouts  15.7 us (6%)
  other arithmetic  7.54 us (3%)
    all_to_all x1, waiting for transfers between devices, local(): lax.all_to_all(copies, 'tp', 0, 0, tiled=True).reshape(-1, normed.shape[1])  63 us
    reduce_scatter x1, waiting for transfers between devices, local(): lax.psum_scatter(jnp.dot(normed_heads, out_columns, preferred_element_typ...  49.7 us
    ppermute x6, starting transfers between devices, shifted(): got = lax.ppermute(message, axis, pairs)  39.4 us
    ppermute x6, waiting for transfers between devices, shifted(): got = lax.ppermute(message, axis, pairs)  20.9 us
    all_gather x1, waiting for transfers between devices, local(): parameter_collection = lax.all_gather(w_qkv, 'ctx', axis=0, tiled=True)  19.3 us
    dot_general x1, matrix products, local(): jnp.dot(every_row_list, parameter_collection, preferred_element_type=jnp....  10.9 us
    all_gather x1, waiting for transfers between devices, local(): out_columns = lax.all_gather(w_out, 'ctx', axis=1, tiled=True)  10.5 us
    all_to_all x1, starting transfers between devices, local(): lax.all_to_all(copies, 'tp', 0, 0, tiled=True).reshape(-1, normed.shape[1])  8.05 us
  transfers between devices with their start and end apart: 10, of which 10 were waited for; matrix products, arithmetic and copies ran while one was open for 14% of the time, Pallas kernels for 0%

commit v1 on v0

--- a/solution.py
+++ b/solution.py
@@ -1,3 +1,4 @@
+import functools
 import jax
 import jax.numpy as jnp
 from jax import lax
@@ -8,6 +9,18 @@
 EPSILON = 1e-06
 FORGET_STEP = 0.5
 INPUT_STEP = 0.5
+
+
+def mix_case(block_here, group_axis):
+    return jnp.concatenate(
+        lax.all_to_all(
+            jnp.stack([block_here for _ in range(lax.axis_size(group_axis))]), group_axis, 0, 0
+        ),
+        axis=0,
+    )
+
+
+_wait_lines = functools.partial(mix_case, group_axis="ctx")
 
 
 def carried_in(passing, state, axis):
@@ -104,7 +117,7 @@
     group = lax.axis_size("tp")
     copies = jnp.broadcast_to(normed[None], (group,) + normed.shape)
     every_row_list = lax.all_to_all(copies, "tp", 0, 0, tiled=True).reshape(-1, normed.shape[1])
-    parameter_collection = lax.all_gather(w_qkv, "ctx", axis=0, tiled=True)
+    parameter_collection = _wait_lines(w_qkv)
     rows_combined = jnp.dot(
         every_row_list, parameter_collection, preferred_element_type=jnp.float32
     )

time: 285 us -> 480 us (1.68)
  waiting for transfers between devices: 165 us -> 280 us
  blocking collectives: 0 us -> 78.8 us
    all_to_all x1, waiting for transfers between devices: 63 us -> 197 us  [mix_case(): lax.all_to_all(jnp.stack([block_here for _ in range(lax.axis_size(group_a...]
    all_to_all x0 -> x1, blocking collectives: none -> 78.8 us  [local(): lax.all_to_all(copies, 'tp', 0, 0, tiled=True).reshape(-1, normed.shape[1])]
    all_gather x1 -> x0, waiting for transfers between devices: 19.3 us -> none  [local(): parameter_collection = lax.all_gather(w_qkv, 'ctx', axis=0, tiled=True)]
    reduce_scatter x1, waiting for transfers between devices: 49.7 us -> 64 us  [local(): lax.psum_scatter(jnp.dot(normed_heads, out_columns, preferred_element_typ...]
    all_gather x1, waiting for transfers between devices: 10.5 us -> 0.02 us  [local(): out_columns = lax.all_gather(w_out, 'ctx', axis=1, tiled=True)]
  transfers between devices with their start and end apart: 10 -> 9, of which waited for: 10 -> 7; matrix products, arithmetic and copies ran while one was open for 14% -> 7% of each run, Pallas kernels for 0% -> 0%
where the time goes in v1:
time: 480 us; the launch traced here: 479 us
  waiting for transfers between devices  280 us (58%)
  blocking collectives  78.8 us (16%)
  starting transfers between devices  46.6 us (10%)
  matrix products  26.6 us (6%)
  between operations  22.2 us (5%)
  local copies, waits for them, and re-layouts  17.5 us (4%)
  other arithmetic  7.94 us (2%)
    all_to_all x1, waiting for transfers between devices, mix_case(): lax.all_to_all(jnp.stack([block_here for _ in range(lax.axis_size(group_a...  197 us
    all_to_all x1, blocking collectives, local(): lax.all_to_all(copies, 'tp', 0, 0, tiled=True).reshape(-1, normed.shape[1])  78.8 us
    reduce_scatter x1, waiting for transfers between devices, local(): lax.psum_scatter(jnp.dot(normed_heads, out_columns, preferred_element_typ...  64 us
    ppermute x6, starting transfers between devices, shifted(): got = lax.ppermute(message, axis, pairs)  35.9 us
    ppermute x6, waiting for transfers between devices, shifted(): got = lax.ppermute(message, axis, pairs)  17.6 us
    dot_general x1, matrix products, local(): jnp.dot(every_row_list, parameter_collection, preferred_element_type=jnp....  10.9 us
    all_to_all x1, starting transfers between devices, mix_case(): lax.all_to_all(jnp.stack([block_here for _ in range(lax.axis_size(group_a...  10.6 us
  transfers between devices with their start and end apart: 9, of which 7 were waited for; matrix products, arithmetic and copies ran while one was open for 7% of the time, Pallas kernels for 0%

profile of v1, /device:TPU:1, one launch (start us, length us, event | category | flops | bytes accessed | tf_op | source)
XLA Modules:
  0.0 479.4 jit_solution(3667016658250359177)
XLA Ops:
  6.5 1.4 fusion.1
  7.9 1.4 fusion.3
  10.1 78.8 %all_to_all.10 = bf16[8,96,4096]{2,1,0:T(8,128)(2,1)} all-to-all(bf16[8,96,4096]{2,1,0:T(8,128)(2,1)S(1)} %broadcast_in_dim.5), channel_id=1, replica_groups=mesh['ctx'=32,'tp'=8] {'tp'}, dimensions={0} | all-to-all | bytes 12582912 | tf_op jit(solution)/shard_map/all_to_all | solution.py:119
  89.0 4.3 stack.4
  93.3 10.6 %all-to-all-start.1 = ((bf16[32,128,1024]{2,1,0:T(8,128)(2,1)}), bf16[32,128,1024]{2,1,0:T(8,128)(2,1)}, u32[]{:S(2)}, u32[]{:S(2)}) async-start(bf16[32,128,1024]{2,1,0:T(8,128)(2,1)} %stack.4), calls=%async_computation.1 | async-start | bytes 16777216 | tf_op jit(solution)/shard_map/all_to_all | solution.py:16
  112.2 197.5 %all-to-all-done.1 = bf16[32,128,1024]{2,1,0:T(8,128)(2,1)} async-done(((bf16[32,128,1024]{2,1,0:T(8,128)(2,1)}), bf16[32,128,1024]{2,1,0:T(8,128)(2,1)}, u32[]{:S(2)}, u32[]{:S(2)}) %all-to-all-start.1) | async-done | bytes 8388640 | tf_op jit(solution)/shard_map/all_to_all | solution.py:16
  309.7 10.9 %convolution_convert_fusion.1 = bf16[768,1024]{1,0:T(8,128)(2,1)S(1)} fusion(bf16[768,4096]{1,0:T(8,128)(2,1)} %bitcast.61, bf16[4096,1024]{1,0:T(8,128)(2,1)} %bitcast.1), kind=kOutput, calls=%fused_computation.7 | convolution fusion | flops 6443237376 | bytes 16252928 | tf_op jit(solution)/shard_map/dot_general | solution.py:121
  321.2 9.3 %collective-permute-start = (bf16[1,272,512]{2,1,0:T(8,128)(2,1)S(1)}, bf16[1,272,512]{2,1,0:T(8,128)(2,1)S(1)}, u32[]{:S(2)}, u32[]{:S(2)}) collective-permute-start(bf16[1,272,512]{2,1,0:T(8,128)(2,1)S(1)} %pad_maximum_fusion), channel_id=1, source_target_pairs={{0,8},{8,16},{16,24},{24,32},{32,40},{40,48},{48,56},{56,64},{64,7... | collective-permute-start | bytes 835592 | tf_op jit(solution)/shard_map/ppermute | solution.py:40
  330.5 3.6 collective-permute-start.1
  334.1 1.9 collective-permute-done
  337.9 4.1 collective-permute-done.1
  345.3 5.6 %collective-permute-start.2 = (bf16[1,272,512]{2,1,0:T(8,128)(2,1)S(1)}, bf16[1,272,512]{2,1,0:T(8,128)(2,1)S(1)}, u32[]{:S(2)}, u32[]{:S(2)}) collective-permute-start(bf16[1,272,512]{2,1,0:T(8,128)(2,1)S(1)} %pad_maximum_fusion.1), channel_id=1, source_target_pairs={{0,16},{8,24},{16,32},{24,40},{32,48},{40,56},{48,64},{56,72},{64,... | collective-permute-start | bytes 835592 | tf_op jit(solution)/shard_map/ppermute | solution.py:40
  351.0 4.6 collective-permute-done.2
  359.0 3.9 collective-permute-start.3
  362.9 3.5 collective-permute-done.3
  368.3 1.3 scatter.45
  369.8 3.6 collective-permute-start.4
  373.4 3.5 collective-permute-done.4
  380.5 10.0 %collective-permute-start.5 = (bf16[1,272,512]{2,1,0:T(8,128)(2,1)S(1)}, bf16[1,272,512]{2,1,0:T(8,128)(2,1)S(1)}, u32[]{:S(2)}, u32[]{:S(2)}) collective-permute-start(bf16[1,272,512]{2,1,0:T(8,128)(2,1)S(1)} %pad_maximum_fusion.4), channel_id=1, source_target_pairs={{0,128},{8,136},{16,144},{24,152},{32,160},{40,168},{48,176},{56,1... | collective-permute-start | bytes 835592 | tf_op jit(solution)/shard_map/ppermute | solution.py:40
  390.5 3.9 fusion.5
  394.4 3.4 fusion.52
  398.5 7.7 %convolution_convert_fusion = bf16[768,4096]{1,0:T(8,128)(2,1)} fusion(bf16[512,4096]{1,0:T(8,128)(2,1)} %all-gather.2.cloned.1.call-done, f32[768,512]{0,1:T(8,128)S(1)} %get-tuple-element.157, f32[512]{0:T(512)S(1)} %copy-done.6, f32[768]{0:T(1024)S(1)} %add_rsqrt_fusion, f32[768]{0:T(1024)S(1)} %broadcast_multiply_fusion), kind=kOutput, calls=%fused_computation | convolution fusion | flops 3225944064 | bytes 12066816 | tf_op jit(solution)/shard_map/dot_general | solution.py:156
  406.3 64.0 %reduce-scatter.2.cloned.1.call-done = bf16[96,4096]{1,0:T(8,128)(2,1)} async-done(((bf16[768,4096]{1,0:T(8,128)(2,1)}), bf16[96,4096]{1,0:T(8,128)(2,1)}) %reduce-scatter.2.cloned.1.call-update) | async-done | bytes 786448 | tf_op jit(solution)/shard_map/reduce_scatter | solution.py:155
  470.3 2.2 fusion.4
  (66 shorter events, 16.2 us)
Async XLA Ops:
  10.1 78.8 %copy-start.1 = (bf16[128,1024]{1,0:T(8,128)(2,1)S(1)}, bf16[128,1024]{1,0:T(8,128)(2,1)}, u32[]{:S(2)}) copy-start(bf16[128,1024]{1,0:T(8,128)(2,1)} %param.35) | copy-start | bytes 786436
  93.2 12.0 %copy-start.5 = (s32[1,768]{1,0:T(1,128)S(1)}, s32[1,768]{1,0:T(1,128)}, u32[]{:S(2)}) copy-start(s32[1,768]{1,0:T(1,128)} %param.39) | copy-start | bytes 9220
  93.3 12.5 %copy-start.3 = (s32[768]{0:T(1024)S(1)}, s32[768]{0:T(1024)}, u32[]{:S(2)}) copy-start(s32[768]{0:T(1024)} %param.41) | copy-start | bytes 9220
  93.3 17.6 %copy-start.4 = (s32[1,768]{1,0:T(1,128)S(1)}, s32[1,768]{1,0:T(1,128)}, u32[]{:S(2)}) copy-start(s32[1,768]{1,0:T(1,128)} %param.38) | copy-start | bytes 9220
  93.3 216.4 %all-to-all-start.1 = ((bf16[32,128,1024]{2,1,0:T(8,128)(2,1)}), bf16[32,128,1024]{2,1,0:T(8,128)(2,1)}, u32[]{:S(2)}, u32[]{:S(2)}) async-start(bf16[32,128,1024]{2,1,0:T(8,128)(2,1)} %stack.4), calls=%async_computation.1 | async-start | bytes 16777216 | tf_op jit(solution)/shard_map/all_to_all | solution.py:16
  103.9 294.2 %all-gather.2.cloned.1.call-start = ((), (), s32[]{:S(2)}) async-start(), calls=%async_computation.3 | async-start | bytes 4325376 | tf_op jit(solution)/shard_map/all_gather | solution.py:154
  104.6 365.7 %reduce-scatter.2.cloned.1.call-start = ((), (), s32[]{:S(2)}) async-start(), calls=%async_computation.4 | async-start | bytes 7077888 | tf_op jit(solution)/shard_map/reduce_scatter | solution.py:155
  320.6 21.4 %copy-start.2 = (bf16[768,1024]{1,0:T(8,128)(2,1)}, bf16[768,1024]{1,0:T(8,128)(2,1)S(1)}, u32[]{:S(2)}) copy-start(bf16[768,1024]{1,0:T(8,128)(2,1)S(1)} %convolution_convert_fusion.1) | copy-start | bytes 4718596
  321.2 14.8 %collective-permute-start = (bf16[1,272,512]{2,1,0:T(8,128)(2,1)S(1)}, bf16[1,272,512]{2,1,0:T(8,128)(2,1)S(1)}, u32[]{:S(2)}, u32[]{:S(2)}) collective-permute-start(bf16[1,272,512]{2,1,0:T(8,128)(2,1)S(1)} %pad_maximum_fusion), channel_id=1, source_target_pairs={{0,8},{8,16},{16,24},{24,32},{32,40},{40,48},{48,56},{56,64},{64,7... | collective-permute-start | bytes 835592 | tf_op jit(solution)/shard_map/ppermute | solution.py:40
  330.5 11.5 %collective-permute-start.1 = (bf16[1,272,512]{2,1,0:T(8,128)(2,1)S(1)}, bf16[1,272,512]{2,1,0:T(8,128)(2,1)S(1)}, u32[]{:S(2)}, u32[]{:S(2)}) collective-permute-start(bf16[1,272,512]{2,1,0:T(8,128)(2,1)S(1)} %pad_maximum_fusion), channel_id=1, source_target_pairs={{0,16},{8,24},{16,32},{24,40},{32,48},{40,56},{48,64},{56,72},{64,... | collective-permute-start | bytes 835592 | tf_op jit(solution)/shard_map/ppermute | solution.py:40
  345.3 10.2 %collective-permute-start.2 = (bf16[1,272,512]{2,1,0:T(8,128)(2,1)S(1)}, bf16[1,272,512]{2,1,0:T(8,128)(2,1)S(1)}, u32[]{:S(2)}, u32[]{:S(2)}) collective-permute-start(bf16[1,272,512]{2,1,0:T(8,128)(2,1)S(1)} %pad_maximum_fusion.1), channel_id=1, source_target_pairs={{0,16},{8,24},{16,32},{24,40},{32,48},{40,56},{48,64},{56,72},{64,... | collective-permute-start | bytes 835592 | tf_op jit(solution)/shard_map/ppermute | solution.py:40
  359.0 7.3 %collective-permute-start.3 = (bf16[1,272,512]{2,1,0:T(8,128)(2,1)S(1)}, bf16[1,272,512]{2,1,0:T(8,128)(2,1)S(1)}, u32[]{:S(2)}, u32[]{:S(2)}) collective-permute-start(bf16[1,272,512]{2,1,0:T(8,128)(2,1)S(1)} %pad_maximum_fusion.2), channel_id=1, source_target_pairs={{0,32},{8,40},{16,48},{24,56},{32,64},{40,72},{48,80},{56,88},{64,... | collective-permute-start | bytes 835592 | tf_op jit(solution)/shard_map/ppermute | solution.py:40
  369.8 7.1 %collective-permute-start.4 = (bf16[1,272,512]{2,1,0:T(8,128)(2,1)S(1)}, bf16[1,272,512]{2,1,0:T(8,128)(2,1)S(1)}, u32[]{:S(2)}, u32[]{:S(2)}) collective-permute-start(bf16[1,272,512]{2,1,0:T(8,128)(2,1)S(1)} %pad_maximum_fusion.3), channel_id=1, source_target_pairs={{0,64},{8,72},{16,80},{24,88},{32,96},{40,104},{48,112},{56,120},{... | collective-permute-start | bytes 835592 | tf_op jit(solution)/shard_map/ppermute | solution.py:40
  380.5 13.9 %collective-permute-start.5 = (bf16[1,272,512]{2,1,0:T(8,128)(2,1)S(1)}, bf16[1,272,512]{2,1,0:T(8,128)(2,1)S(1)}, u32[]{:S(2)}, u32[]{:S(2)}) collective-permute-start(bf16[1,272,512]{2,1,0:T(8,128)(2,1)S(1)} %pad_maximum_fusion.4), channel_id=1, source_target_pairs={{0,128},{8,136},{16,144},{24,152},{32,160},{40,168},{48,176},{56,1... | collective-permute-start | bytes 835592 | tf_op jit(solution)/shard_map/ppermute | solution.py:40
  397.8 0.7 copy-start.6
  406.3 64.1 %copy-start = (bf16[96,4096]{1,0:T(8,128)(2,1)S(1)}, bf16[96,4096]{1,0:T(8,128)(2,1)}, u32[]{:S(2)}) copy-start(bf16[96,4096]{1,0:T(8,128)(2,1)} %param.33) | copy-start | bytes 2359300
Sparse Core Ops, SparseCore 0:
  107.2 193.1 all-gather.1
  406.4 63.8 reduce-scatter.1
